TPU v7x, 32 devices: a whole 2x2x4 slice. The times are simulated.
32 devices in a mesh: gx: 4 (over z), gy: 4 (over y, x), gz: 2 (over core).
Axes of the slice: x: 2, y: 2, z: 4, core: 2. Of those that a mesh axis runs over, the one named last changes fastest.
Arguments:
- params: float32 [59, 65536], P(None, ('gx', 'gy', 'gz')), may hold values from -6 to 6
- gradients: float32 [59, 65536], P(None, ('gx', 'gy', 'gz')), may hold values from -80 to 80
- moment_one: float32 [59, 65536], P(None, ('gx', 'gy', 'gz')), may hold values from -4 to 4
- moment_two: float32 [59, 65536], P(None, ('gx', 'gy', 'gz')), may hold values from 0.01 to 1
- keep_mask: int32 [65536], P(('gx', 'gy', 'gz')), may hold values from 0 to 1, as said below
Outputs:
- new_params: float32 [59, 65536], P(None, ('gx', 'gy', 'gz'))
- new_moment_one: float32 [59, 65536], P(None, ('gx', 'gy', 'gz'))
- new_moment_two: float32 [59, 65536], P(None, ('gx', 'gy', 'gz'))
- grad_rms: float32 [], replicated
Inputs may be any that keep to these rules, and one draw needn't show every extreme that they name: `keep_mask`: exactly 32 of the blocks of 128 aligned columns hold no 1; every other block holds at least one.
All inputs are finite; a program needn't handle non-finite values.
Results may differ from a plain program's by a relative error of at most 0.000067.
Values sent between devices are 32-bit elements; how exact they have to be, the bound alone decides.
A program may use at most 64 MiB of HBM per device.

v0:
```python
import jax
import jax.numpy as jnp
from jax import lax
from jax.sharding import PartitionSpec as P

FEATURES = 59
BLOCK = 128
MOVES = 2
STEP = 10


beta_one = 0.9
beta_two = 0.999
learn_rate = 0.05
adam_eps = 1e-08
clip_rms = 1.0


def passed_along(block, axis, distance):
    devices = range(lax.axis_size(axis))
    route = [(i - distance, i) for i in devices if i - distance in devices]
    return lax.ppermute(block, axis, route)


def adam_update(params, gradients, moment_one, moment_two, clip_factor):
    clipped = clip_factor * gradients
    first = beta_one * moment_one + (1.0 - beta_one) * clipped
    second = beta_two * moment_two + (1.0 - beta_two) * clipped * clipped
    correct_one = 1.0 - beta_one**STEP
    correct_two = 1.0 - beta_two**STEP
    updated = params - learn_rate * (first / correct_one) / (
        jnp.sqrt(second / correct_two) + adam_eps
    )
    return (updated, first, second)


def relocate(stacked, table, blocks_dev):
    members = stacked.shape[0]
    flat_data = stacked.reshape(members * FEATURES, blocks_dev, BLOCK)
    window = jnp.einsum("anr,nw->awr", flat_data, table, precision=lax.Precision.HIGHEST)
    result = window[:, MOVES * blocks_dev : (MOVES + 1) * blocks_dev]
    for distance in range(1, MOVES + 1):
        outgoing = window[:, (MOVES - distance) * blocks_dev : (MOVES - distance + 1) * blocks_dev]
        result = result + passed_along(outgoing, ("gx", "gy", "gz"), -distance)
    return result.reshape(members, FEATURES, blocks_dev * BLOCK)


def shards(params, gradients, moment_one, moment_two, keep_mask):
    row_count = params.shape[1]
    blocks_dev = row_count // BLOCK
    devices_all = lax.axis_size(("gx", "gy", "gz"))
    my_index = lax.axis_index(("gx", "gy", "gz"))
    local_square = jnp.sum(gradients * gradients)
    counts = jnp.sum(keep_mask.reshape(blocks_dev, BLOCK), axis=1)
    block_alive = (counts > 0).astype(jnp.int32)
    local_alive = jnp.sum(block_alive)
    squares_all, alive_all = (
        lax.all_gather(local_square[None], ("gx", "gy", "gz"), axis=0, tiled=True),
        lax.all_gather(local_alive[None], ("gx", "gy", "gz"), axis=0, tiled=True),
    )
    square_total = jnp.sum(squares_all)
    lower = jnp.arange(devices_all, dtype=jnp.int32) < my_index
    offset = jnp.sum(jnp.where(lower, alive_all, 0)).astype(jnp.int32)
    grad_rms = jnp.sqrt(square_total / (FEATURES * row_count * devices_all))
    clip_factor = jnp.minimum(1.0, clip_rms / (grad_rms + 1e-06))
    local_rank = jnp.cumsum(block_alive) - block_alive
    window_slot = offset + local_rank - (my_index - MOVES) * blocks_dev
    window_blocks = (MOVES + 1) * blocks_dev
    columns = jnp.arange(window_blocks, dtype=jnp.int32)[None, :]
    table = ((columns == window_slot[:, None]) & (block_alive[:, None] > 0)).astype(jnp.float32)
    kept_rows = keep_mask[None, None, :] > 0
    updated, first, second = adam_update(params, gradients, moment_one, moment_two, clip_factor)
    stacked = jnp.where(kept_rows, jnp.stack([updated, first, second]), 0.0)
    moved = relocate(stacked, table, blocks_dev)
    return (moved[0], moved[1], moved[2], grad_rms)


def solution(mesh):
    in_specs = (
        P(None, ("gx", "gy", "gz")),
        P(None, ("gx", "gy", "gz")),
        P(None, ("gx", "gy", "gz")),
        P(None, ("gx", "gy", "gz")),
        P(("gx", "gy", "gz")),
    )
    out_specs = (
        P(None, ("gx", "gy", "gz")),
        P(None, ("gx", "gy", "gz")),
        P(None, ("gx", "gy", "gz")),
        P(),
    )
    return jax.shard_map(shards, mesh=mesh, in_specs=in_specs, out_specs=out_specs, check_vma=False)
```

profile of v0, /device:TPU:0, one launch (start us, length us, event | category | flops | bytes accessed | tf_op | source)
XLA Modules:
  0.0 152.2 jit_solution(2894387770556503537)
XLA Ops:
  0.6 0.8 bitcast_reduce_fusion
  1.4 0.6 fusion.15
  2.1 0.7 compare_bitcast_fusion
  2.8 1.8 %multiply_reduce_fusion = f32[]{:T(128)} fusion(f32[59,2048]{1,0:T(8,128)} %param.6), kind=kLoop, calls=%fused_computation.11 | loop fusion | flops 241663 | bytes 483332 | tf_op jit(solution)/shard_map/reduce_sum | solution.py:53
  4.6 0.8 dynamic-update-slice
  5.3 41.9 %all-reduce = s32[32]{0:T(128)S(1)} all-reduce(s32[32]{0:T(128)S(1)} %dynamic-update-slice), channel_id=1, replica_groups=mesh['gx'=4,'gy'=4,'gz'=2] {'gx','gy','gz'}, use_global_device_ids=true, to_apply=%add | all-reduce | flops 32 | bytes 256
  47.3 0.6 fusion.12
  47.9 0.8 dynamic-update-slice.1
  48.7 40.0 %all-reduce.1 = f32[32]{0:T(128)S(1)} all-reduce(f32[32]{0:T(128)S(1)} %dynamic-update-slice.1), channel_id=1, replica_groups=mesh['gx'=4,'gy'=4,'gz'=2] {'gx','gy','gz'}, use_global_device_ids=true, to_apply=%add.1 | all-reduce | flops 32 | bytes 256
  88.7 0.6 reduce_sum.49
  90.0 0.1 copy.11
  90.2 0.1 reduce.1
  90.3 1.9 %subtract_bitcast_fusion = (f32[1,59,2048]{2,1,0:T(8,128)S(1)}, f32[1,59,2048]{2,1,0:T(8,128)S(1)}, f32[1,59,2048]{2,1,0:T(8,128)S(1)}) fusion(f32[59,2048]{1,0:T(8,128)} %param.5, f32[59,2048]{1,0:T(8,128)} %param.6, f32[]{:T(128)S(6)} %min.3, f32[59,2048]{1,0:T(8,128)} %param.7, f32[59,2048]{1,0:T(8,128)} %param.8), kind=kLoop, calls=%fused_computation.9 | loop fusion | flops 1570816 | bytes 3383300 | tf_op jit(solution)/shard_map/stack | solution.py:73
  92.2 0.1 pad_maximum_fusion
  92.3 0.2 stack.18
  92.5 0.7 add_subtract_fusion
  93.2 2.0 %convolution_bitcast_fusion = f32[177,48,128]{2,1,0:T(8,128)S(1)} fusion(f32[177,16,128]{2,1,0:T(8,128)S(1)} %stack.18, pred[16,128]{1,0:T(8,128)(4,1)S(1)} %compare_bitcast_fusion, s32[16]{0:T(128)S(1)} %add_subtract_fusion, pred[16]{0:T(512)(128)(4,1)S(1)} %get-tuple-element.12), kind=kOutput, calls=%fused_computation | convolution fusion | flops 209161728 | bytes 5802064 | tf_op jit(solution)/shard_map/anr,nw->awr/dot_general | solution.py:40
  95.2 0.2 fusion.16
  95.4 1.3 collective-permute-start
  96.7 1.3 collective-permute-start.1
  98.0 2.5 %collective-permute-done = f32[177,16,128]{2,1,0:T(8,128)S(1)} collective-permute-done((f32[177,16,128]{2,1,0:T(8,128)S(1)}, f32[177,16,128]{2,1,0:T(8,128)S(1)}, u32[]{:S(2)}, u32[]{:S(2)}) %collective-permute-start) | collective-permute-done | bytes 1450016 | tf_op jit(solution)/shard_map/ppermute | solution.py:22
  100.5 47.2 %collective-permute-done.1 = f32[177,16,128]{2,1,0:T(8,128)S(1)} collective-permute-done((f32[177,16,128]{2,1,0:T(8,128)S(1)}, f32[177,16,128]{2,1,0:T(8,128)S(1)}, u32[]{:S(2)}, u32[]{:S(2)}) %collective-permute-start.1) | collective-permute-done | bytes 1450016 | tf_op jit(solution)/shard_map/ppermute | solution.py:22
  147.7 0.3 fusion
  148.0 0.1 fusion.17
  148.1 1.0 copy.14
  149.1 1.0 copy.13
  150.1 1.0 copy.12
  (7 shorter events, 0.2 us)
Async XLA Ops:
  95.4 5.1 %collective-permute-start = (f32[177,16,128]{2,1,0:T(8,128)S(1)}, f32[177,16,128]{2,1,0:T(8,128)S(1)}, u32[]{:S(2)}, u32[]{:S(2)}) collective-permute-start(f32[177,16,128]{2,1,0:T(8,128)S(1)} %get-tuple-element.4), channel_id=1, source_target_pairs={{1,0},{2,1},{3,2},{4,3},{5,4},{6,5},{7,6},{8,7},{9,8},{10,9},{11,1... | collective-permute-start | bytes 4349960 | tf_op jit(solution)/shard_map/ppermute | solution.py:22
  96.7 51.0 %collective-permute-start.1 = (f32[177,16,128]{2,1,0:T(8,128)S(1)}, f32[177,16,128]{2,1,0:T(8,128)S(1)}, u32[]{:S(2)}, u32[]{:S(2)}) collective-permute-start(f32[177,16,128]{2,1,0:T(8,128)S(1)} %get-tuple-element.5), channel_id=1, source_target_pairs={{2,0},{3,1},{4,2},{5,3},{6,4},{7,5},{8,6},{9,7},{10,8},{11,9},{12,... | collective-permute-start | bytes 4349960 | tf_op jit(solution)/shard_map/ppermute | solution.py:22
where the time goes:
time: 153 us; the launch traced here: 152 us
  blocking collectives  82 us (54%)
  waiting for transfers between devices  49.7 us (32%)
  other arithmetic  8.25 us (5%)
  local copies, waits for them, and re-layouts  5.08 us (3%)
  between operations  2.59 us (2%)
  starting transfers between devices  2.58 us (2%)
  matrix products  1.97 us (1%)
    unnamed x2, blocking collectives  82 us
    ppermute x2, waiting for transfers between devices, passed_along(): return lax.ppermute(block, axis, route)  49.7 us
    unnamed x10, local copies, waits for them, and re-layouts  4.48 us
  transfers between devices with their start and end apart: 2, of which 2 were waited for; matrix products, arithmetic and copies ran while one was open for 0% of the time, Pallas kernels for 0%

commit v1 on v0

v1 whole, which is shorter than its diff:
```python
import functools

import jax
import jax.numpy as jnp
from jax import lax
from jax.experimental import pallas as pl
from jax.experimental.pallas import tpu as pltpu
from jax.sharding import PartitionSpec as P

BLOCK = 128
DROPS = 32
STEP = 10
AXES = ("gx", "gy", "gz")
MESH = pl.DeviceIdType.MESH

beta_one = 0.9
beta_two = 0.999
learn_rate = 0.05
adam_eps = 1e-08
clip_rms = 1.0


def kernel(
    sizes, pieces, p_hbm, g_hbm, m_hbm, v_hbm, k_hbm, op_hbm, om_hbm, ov_hbm, rms_ref,
    windows, g_buf, m_buf, v_buf, o_p, o_m, o_v, keep, ag_x, ag_y, ag_z, ct_x, ct_y, ct_z,
    where_v, where_s, load_sem, out_sem, far_send, far_recv, near_send, near_recv,
    ag_send, ag_recv, where_sem,
):
    nx, ny, nz = sizes
    count = nx * ny * nz
    features, rows_dev = g_buf.shape
    blocks_dev = rows_dev // BLOCK
    n_piece = len(pieces)
    ix, iy, iz = (lax.axis_index(a) for a in AXES)
    me = (ix * ny + iy) * nz + iz
    odd = lax.rem(me, 2)
    is_odd = odd == 1
    is_even = odd == 0
    has_up = me + 2 < count
    has_down = me >= 2

    def place(n):
        return (lax.div(n, ny * nz), lax.rem(lax.div(n, nz), ny), lax.rem(n, nz))

    partner = place(me + 1 - 2 * odd)
    below = place(lax.rem(me + count - 2, count))
    above = place(lax.rem(me + 2, count))
    own, one, two = (pl.ds(i * rows_dev, rows_dev) for i in range(3))

    def span(piece):
        return pl.ds(pieces[piece][0], pieces[piece][1])

    def load(i, src, dst):
        return pltpu.make_async_copy(src, dst, load_sem.at[i])

    loads = [
        load(0, g_hbm, g_buf),
        load(1, k_hbm, keep.at[0]),
        load(2, m_hbm, m_buf),
        load(3, v_hbm, v_buf),
    ] + [
        load(4 + c, p_hbm.at[span(c)], windows[0][c].at[:, own]) for c in range(len(pieces))
    ]
    for c in loads:
        c.start()

    barrier = pltpu.get_barrier_semaphore()

    def greet(device):
        pl.semaphore_signal(barrier, inc=1, device_id=device, device_id_type=MESH)

    groups = (
        (iz, nz, ag_z, ct_z, lambda i: (ix, iy, i)),
        (iy, ny, ag_y, ct_y, lambda i: (ix, i, iz)),
        (ix, nx, ag_x, ct_x, lambda i: (i, iy, iz)),
    )
    greet(partner)
    for mine, size, _, _, at in groups:
        for k in range(1, size):
            greet(at(lax.rem(mine + k, size)))
    pl.when(has_down)(lambda: greet(below))
    pl.when(has_up)(lambda: greet(above))

    loads[0].wait()
    loads[1].wait()
    g = g_buf[...]
    square = jnp.sum(g * g, axis=1, keepdims=True)
    square = jnp.sum(square, axis=0, keepdims=True)
    alive = (jnp.max(keep[0], axis=1, keepdims=True) > 0).astype(jnp.int32)
    payload = jnp.broadcast_to(square, (8, BLOCK))
    tally = jnp.broadcast_to(jnp.sum(alive, axis=0, keepdims=True), (8, BLOCK))

    pl.semaphore_wait(
        barrier,
        1 + (nx - 1) + (ny - 1) + (nz - 1) + has_up.astype(jnp.int32) + has_down.astype(jnp.int32),
    )

    def far(i, src, dst):
        return pltpu.make_async_remote_copy(
            src_ref=src, dst_ref=dst, send_sem=far_send.at[i], recv_sem=far_recv.at[i],
            device_id=below, device_id_type=MESH,
        )

    def near(i, src, dst):
        return pltpu.make_async_remote_copy(
            src_ref=src, dst_ref=dst, send_sem=near_send.at[i], recv_sem=near_recv.at[i],
            device_id=partner, device_id_type=MESH,
        )

    keep_id = 3 * n_piece

    def far_copy(a, c):
        src = p_hbm.at[span(c)] if a == 0 else windows[a][c].at[:, own]
        return far(a * n_piece + c, src, windows[a][c].at[:, two])

    def near_own(a, c):
        src = p_hbm.at[span(c)] if a == 0 else windows[a][c].at[:, own]
        return near(a * n_piece + c, src, windows[a][c].at[:, one])

    def near_relay(a, c):
        return near(a * n_piece + c, windows[a][c].at[:, two], windows[a][c].at[:, one])

    far_keep = far(keep_id, k_hbm, keep.at[2])
    near_keep = near(keep_id, k_hbm, keep.at[1])
    relay_keep = near(keep_id, keep.at[2], keep.at[1])

    def send(a, c):
        pl.when(has_down)(lambda: far_copy(a, c).start())
        pl.when(is_odd)(lambda: near_own(a, c).start())

    pl.when(has_down)(far_keep.start)
    pl.when(is_odd)(near_keep.start)

    def no_keep(i):
        keep[i] = jnp.zeros((blocks_dev, BLOCK), jnp.int32)

    pl.when(jnp.logical_not(has_up))(lambda: no_keep(2))
    pl.when(jnp.logical_not(has_up) & is_odd)(lambda: no_keep(1))

    before = jnp.zeros((8, BLOCK), jnp.int32)
    flow = list(range(n_piece))
    sem_at = 0
    ag_copies = []
    for phase, (mine, size, ag, ct, at) in enumerate(groups):
        ag[mine] = payload
        ct[mine] = tally
        copies = []
        for k in range(1, size):
            for buf in (ag, ct):
                copies.append(
                    pltpu.make_async_remote_copy(
                        src_ref=buf.at[mine], dst_ref=buf.at[mine],
                        send_sem=ag_send.at[sem_at], recv_sem=ag_recv.at[sem_at],
                        device_id=at(lax.rem(mine + k, size)), device_id_type=MESH,
                    )
                )
                copies[-1].start()
                sem_at += 1
        for _ in range(1 if phase < 2 else n_piece):
            if flow:
                send(0, flow.pop(0))
        for c in copies:
            c.wait_recv()
        ag_copies += copies
        payload, tally = ag[0], ct[0]
        for i in range(1, size):
            payload, tally = payload + ag[i], tally + ct[i]
        for i in range(size):
            before = before + jnp.where(i < mine, ct[i], 0)

    grad_rms = jnp.sqrt(payload[0:1, 0:1] / float(features * rows_dev * count))
    rms_ref[...] = grad_rms
    clip_factor = jnp.minimum(1.0, clip_rms / (grad_rms + 1e-06))

    loads[2].wait()
    loads[3].wait()
    kept = keep[0]
    kept = jnp.concatenate([kept[b : b + 1, :] for b in range(blocks_dev)], axis=1) > 0
    for c in range(n_piece):
        rows = span(c)
        clipped = clip_factor * g_buf[rows, :]
        first = beta_one * m_buf[rows, :] + (1.0 - beta_one) * clipped
        windows[1][c][:, own] = jnp.where(kept, first, 0.0)
        second = beta_two * v_buf[rows, :] + (1.0 - beta_two) * clipped * clipped
        windows[2][c][:, own] = jnp.where(kept, second, 0.0)
        send(1, c)
        send(2, c)

    @pl.when(has_up)
    def _():
        far_keep.wait_recv()

    @pl.when(is_even & has_up)
    def _():
        relay_keep.start()

    pl.when(is_even | has_up)(near_keep.wait_recv)
    total_blocks = 3 * blocks_dev
    flags = [(jnp.max(keep[i], axis=1, keepdims=True) > 0).astype(jnp.int32) for i in range(3)]
    flags = jnp.concatenate(flags, axis=0)
    up_to = lax.broadcasted_iota(jnp.int32, (total_blocks, BLOCK), 0) <= lax.broadcasted_iota(
        jnp.int32, (total_blocks, BLOCK), 1
    )
    reached = jnp.sum(
        jnp.where(up_to, jnp.broadcast_to(flags, (total_blocks, BLOCK)), 0), axis=0, keepdims=True
    )
    shift = me * blocks_dev - before[0:1, :]
    slot = lax.broadcasted_iota(jnp.int32, (blocks_dev, BLOCK), 0)
    lane = lax.broadcasted_iota(jnp.int32, (blocks_dev, BLOCK), 1)
    passed = (reached <= slot + shift) & (lane < total_blocks)
    index = jnp.sum(passed.astype(jnp.int32), axis=1, keepdims=True)
    where_v[...] = jnp.broadcast_to(index, (blocks_dev, BLOCK))
    to_scalar = pltpu.make_async_copy(where_v, where_s, where_sem)
    to_scalar.start()
    to_scalar.wait()
    for c in loads[4:]:
        c.wait()

    def relay(a, c):
        @pl.when(has_up)
        def _():
            far_copy(a, c).wait_recv()

        @pl.when(is_even & has_up)
        def _():
            near_relay(a, c).start()

    for c in range(n_piece):
        relay(0, c)

    correct_one = 1.0 - beta_one**STEP
    correct_two = 1.0 - beta_two**STEP
    outs = []
    for c in range(n_piece):
        relay(1, c)
        relay(2, c)
        for a in range(3):
            pl.when(is_even | has_up)(near_own(a, c).wait_recv)
        rows = span(c)
        for j in range(blocks_dev):
            block = where_s[j, 0]
            valid = block < total_blocks
            start = jnp.where(valid, block, 0) * BLOCK
            dst = (rows, pl.ds(j * BLOCK, BLOCK))
            old, first, second = (windows[a][c][:, pl.ds(start, BLOCK)] for a in range(3))
            updated = old - learn_rate * (first / correct_one) / (
                jnp.sqrt(second / correct_two) + adam_eps
            )
            o_p[dst] = jnp.where(valid & (second > 0.0), updated, 0.0)
            o_m[dst] = jnp.where(valid, first, 0.0)
            o_v[dst] = jnp.where(valid, second, 0.0)
        for a, (buf, hbm) in enumerate(((o_p, op_hbm), (o_m, om_hbm), (o_v, ov_hbm))):
            outs.append(
                pltpu.make_async_copy(buf.at[rows], hbm.at[rows], out_sem.at[a * n_piece + c])
            )
            outs[-1].start()

    @pl.when(has_down)
    def _():
        far_keep.wait_send()
        for a in range(3):
            for c in range(n_piece):
                far_copy(a, c).wait_send()

    @pl.when(is_odd | has_up)
    def _():
        near_keep.wait_send()
        for a in range(3):
            for c in range(n_piece):
                near_own(a, c).wait_send()

    for c in ag_copies:
        c.wait_send()
    for c in outs:
        c.wait()


def shards(params, gradients, moment_one, moment_two, keep_mask):
    features, rows_dev = params.shape
    blocks_dev = rows_dev // BLOCK
    sizes = tuple(lax.axis_size(a) for a in AXES)
    assert DROPS <= 2 * blocks_dev and sizes[2] % 2 == 0
    step = 16
    pieces = [(r, min(step, features - r)) for r in range(0, features, step)]
    full = jax.ShapeDtypeStruct((features, rows_dev), jnp.float32)
    plain = pltpu.VMEM((features, rows_dev), jnp.float32)
    window = [pltpu.VMEM((rows, 3 * rows_dev), jnp.float32) for _, rows in pieces]
    n_piece = len(pieces)
    n_ag = 2 * (sum(sizes) - 3)
    any_spec = pl.BlockSpec(memory_space=pl.ANY)
    p1, m1, v1, rms = pl.pallas_call(
        functools.partial(kernel, sizes, pieces),
        out_shape=(full, full, full, jax.ShapeDtypeStruct((1, 1), jnp.float32)),
        in_specs=[any_spec] * 5,
        out_specs=(any_spec, any_spec, any_spec, pl.BlockSpec(memory_space=pltpu.VMEM)),
        scratch_shapes=[
            [window, window, window], plain, plain, plain, plain, plain, plain,
            pltpu.VMEM((3, blocks_dev, BLOCK), jnp.int32),
            pltpu.VMEM((sizes[0], 8, BLOCK), jnp.float32),
            pltpu.VMEM((sizes[1], 8, BLOCK), jnp.float32),
            pltpu.VMEM((sizes[2], 8, BLOCK), jnp.float32),
            pltpu.VMEM((sizes[0], 8, BLOCK), jnp.int32),
            pltpu.VMEM((sizes[1], 8, BLOCK), jnp.int32),
            pltpu.VMEM((sizes[2], 8, BLOCK), jnp.int32),
            pltpu.VMEM((blocks_dev, BLOCK), jnp.int32),
            pltpu.SMEM((blocks_dev, BLOCK), jnp.int32),
            pltpu.SemaphoreType.DMA((4 + n_piece,)),
            pltpu.SemaphoreType.DMA((3 * n_piece,)),
            pltpu.SemaphoreType.DMA((3 * n_piece + 1,)),
            pltpu.SemaphoreType.DMA((3 * n_piece + 1,)),
            pltpu.SemaphoreType.DMA((3 * n_piece + 1,)),
            pltpu.SemaphoreType.DMA((3 * n_piece + 1,)),
            pltpu.SemaphoreType.DMA((n_ag,)),
            pltpu.SemaphoreType.DMA((n_ag,)),
            pltpu.SemaphoreType.DMA,
        ],
        compiler_params=pltpu.CompilerParams(
            collective_id=0, has_side_effects=True, vmem_limit_bytes=40 * 1024 * 1024
        ),
    )(params, gradients, moment_one, moment_two, keep_mask.reshape(blocks_dev, BLOCK))
    return p1, m1, v1, rms.reshape(())


def solution(mesh):
    spec = P(None, AXES)
    return jax.shard_map(
        shards, mesh=mesh, in_specs=(spec, spec, spec, spec, P(AXES)),
        out_specs=(spec, spec, spec, P()), check_vma=False,
    )
```

time: 153 us -> 57.5 us (0.38)
  the two profiles are of different devices: /device:TPU:0 before, /device:TPU:5 now
where the time goes in v1:
time: 57.5 us; the launch traced here: 57.1 us
  Pallas kernels  47.6 us (83%)
  local copies, waits for them, and re-layouts  7.24 us (13%)
  between operations  2.34 us (4%)
    pallas_call x1, Pallas kernels, shards(): pl.pallas_call(functools.partial(kernel, sizes, pieces), out_shape=(full,...  47.6 us
    unnamed x13, local copies, waits for them, and re-layouts  7.24 us

profile of v1, /device:TPU:5, one launch (start us, length us, event | category | flops | bytes accessed | tf_op | source)
XLA Modules:
  0.0 57.1 jit_solution(14354132429206386662)
XLA Ops:
  0.6 0.0 copy-start
  0.6 1.0 %copy-done = f32[59,2048]{1,0:T(8,128)S(1)} copy-done((f32[59,2048]{1,0:T(8,128)S(1)}, f32[59,2048]{1,0:T(8,128)}, u32[]{:S(2)}) %copy-start) | copy-done | bytes 483352
  1.7 0.0 copy-start.1
  1.7 1.0 %copy-done.1 = f32[59,2048]{1,0:T(8,128)S(1)} copy-done((f32[59,2048]{1,0:T(8,128)S(1)}, f32[59,2048]{1,0:T(8,128)}, u32[]{:S(2)}) %copy-start.1) | copy-done | bytes 483352
  2.7 0.0 copy-start.2
  2.7 1.0 %copy-done.2 = f32[59,2048]{1,0:T(8,128)S(1)} copy-done((f32[59,2048]{1,0:T(8,128)S(1)}, f32[59,2048]{1,0:T(8,128)}, u32[]{:S(2)}) %copy-start.2) | copy-done | bytes 483352
  3.8 0.0 copy-start.3
  3.8 1.0 %copy-done.3 = f32[59,2048]{1,0:T(8,128)S(1)} copy-done((f32[59,2048]{1,0:T(8,128)S(1)}, f32[59,2048]{1,0:T(8,128)}, u32[]{:S(2)}) %copy-start.3) | copy-done | bytes 483352
  4.8 0.0 copy-start.4
  4.8 0.7 %copy-done.4 = s32[2048]{0:T(1024)S(1)} copy-done((s32[2048]{0:T(1024)S(1)}, s32[2048]{0:T(1024)}, u32[]{:S(2)}) %copy-start.4) | copy-done | bytes 8216
  5.5 47.6 %shard_map.84 = (f32[59,2048]{1,0:T(8,128)S(1)}, f32[59,2048]{1,0:T(8,128)S(1)}, f32[59,2048]{1,0:T(8,128)S(1)}, f32[1,1]{1,0:T(1,128)}) custom-call(f32[59,2048]{1,0:T(8,128)S(1)} %copy-done, f32[59,2048]{1,0:T(8,128)S(1)} %copy-done.1, f32[59,2048]{1,0:T(8,128)S(1)} %copy-done.2, f32[59,2048]{1,0:T(8,128)S(1)} %copy-done.3, s32[16,128]{1,0:T(8,128)S(1)} %bitcast.2), custom_call_target="tpu_custom_call" | custom-call | tf_op jit(solution)/shard_map/pallas_call | solution.py:291
  53.1 0.8 %copy.13 = f32[59,2048]{1,0:T(8,128)} copy(f32[59,2048]{1,0:T(8,128)S(1)} %get-tuple-element.16) | data formatting | bytes 966656
  53.9 0.8 %copy.14 = f32[59,2048]{1,0:T(8,128)} copy(f32[59,2048]{1,0:T(8,128)S(1)} %get-tuple-element.17) | data formatting | bytes 966656
  54.7 0.8 %copy.15 = f32[59,2048]{1,0:T(8,128)} copy(f32[59,2048]{1,0:T(8,128)S(1)} %get-tuple-element.18) | data formatting | bytes 966656
Async XLA Ops:
  0.6 1.0 %copy-start = (f32[59,2048]{1,0:T(8,128)S(1)}, f32[59,2048]{1,0:T(8,128)}, u32[]{:S(2)}) copy-start(f32[59,2048]{1,0:T(8,128)} %p_hbm.1) | copy-start | bytes 1449988
  1.7 1.0 %copy-start.1 = (f32[59,2048]{1,0:T(8,128)S(1)}, f32[59,2048]{1,0:T(8,128)}, u32[]{:S(2)}) copy-start(f32[59,2048]{1,0:T(8,128)} %g_hbm.1) | copy-start | bytes 1449988
  2.7 1.0 %copy-start.2 = (f32[59,2048]{1,0:T(8,128)S(1)}, f32[59,2048]{1,0:T(8,128)}, u32[]{:S(2)}) copy-start(f32[59,2048]{1,0:T(8,128)} %m_hbm.1) | copy-start | bytes 1449988
  3.8 1.0 %copy-start.3 = (f32[59,2048]{1,0:T(8,128)S(1)}, f32[59,2048]{1,0:T(8,128)}, u32[]{:S(2)}) copy-start(f32[59,2048]{1,0:T(8,128)} %v_hbm.1) | copy-start | bytes 1449988
  4.8 0.7 %copy-start.4 = (s32[2048]{0:T(1024)S(1)}, s32[2048]{0:T(1024)}, u32[]{:S(2)}) copy-start(s32[2048]{0:T(1024)} %param.9) | copy-start | bytes 24580

commit v2 on v1

--- a/solution.py
+++ b/solution.py
@@ -8,6 +8,7 @@
 from jax.sharding import PartitionSpec as P
 
 BLOCK = 128
+ROWS = 8
 DROPS = 32
 STEP = 10
 AXES = ("gx", "gy", "gz")
@@ -21,9 +22,9 @@
 
 
 def kernel(
-    sizes, pieces, p_hbm, g_hbm, m_hbm, v_hbm, k_hbm, op_hbm, om_hbm, ov_hbm, rms_ref,
-    windows, g_buf, m_buf, v_buf, o_p, o_m, o_v, keep, ag_x, ag_y, ag_z, ct_x, ct_y, ct_z,
-    where_v, where_s, load_sem, out_sem, far_send, far_recv, near_send, near_recv,
+    sizes, pieces, p_hbm, g_hbm, m_hbm, v_hbm, k_hbm, o_p, o_m, o_v, rms_ref,
+    windows, tails, g_buf, m_buf, v_buf, p_rest, keep, ag_x, ag_y, ag_z, ct_x, ct_y, ct_z,
+    where_v, where_s, load_sem, far_send, far_recv, near_send, near_recv,
     ag_send, ag_recv, where_sem,
 ):
     nx, ny, nz = sizes
@@ -31,6 +32,8 @@
     features, rows_dev = g_buf.shape
     blocks_dev = rows_dev // BLOCK
     n_piece = len(pieces)
+    rest = p_rest.shape[0]
+    top = features - rest
     ix, iy, iz = (lax.axis_index(a) for a in AXES)
     me = (ix * ny + iy) * nz + iz
     odd = lax.rem(me, 2)
@@ -45,7 +48,7 @@
     partner = place(me + 1 - 2 * odd)
     below = place(lax.rem(me + count - 2, count))
     above = place(lax.rem(me + 2, count))
-    own, one, two = (pl.ds(i * rows_dev, rows_dev) for i in range(3))
+    own = pl.ds(0, rows_dev)
 
     def span(piece):
         return pl.ds(pieces[piece][0], pieces[piece][1])
@@ -60,7 +63,7 @@
         load(3, v_hbm, v_buf),
     ] + [
         load(4 + c, p_hbm.at[span(c)], windows[0][c].at[:, own]) for c in range(len(pieces))
-    ]
+    ] + [load(4 + n_piece, p_hbm.at[pl.ds(top, rest)], p_rest)]
     for c in loads:
         c.start()
 
@@ -107,18 +110,24 @@
             device_id=partner, device_id_type=MESH,
         )
 
-    keep_id = 3 * n_piece
+    keep_id = 3 * n_piece + 3
+
+    def place_of(a, c, slot):
+        if c < n_piece:
+            return windows[a][c].at[:, pl.ds(slot * rows_dev, rows_dev)]
+        return tails[a].at[:, pl.ds(slot * blocks_dev, blocks_dev), :]
+
+    def mine_of(a, c):
+        return p_hbm.at[span(c)] if a == 0 and c < n_piece else place_of(a, c, 0)
 
     def far_copy(a, c):
-        src = p_hbm.at[span(c)] if a == 0 else windows[a][c].at[:, own]
-        return far(a * n_piece + c, src, windows[a][c].at[:, two])
+        return far(a * (n_piece + 1) + c, mine_of(a, c), place_of(a, c, 2))
 
     def near_own(a, c):
-        src = p_hbm.at[span(c)] if a == 0 else windows[a][c].at[:, own]
-        return near(a * n_piece + c, src, windows[a][c].at[:, one])
+        return near(a * (n_piece + 1) + c, mine_of(a, c), place_of(a, c, 1))
 
     def near_relay(a, c):
-        return near(a * n_piece + c, windows[a][c].at[:, two], windows[a][c].at[:, one])
+        return near(a * (n_piece + 1) + c, place_of(a, c, 2), place_of(a, c, 1))
 
     far_keep = far(keep_id, k_hbm, keep.at[2])
     near_keep = near(keep_id, k_hbm, keep.at[1])
@@ -185,6 +194,26 @@
         windows[2][c][:, own] = jnp.where(kept, second, 0.0)
         send(1, c)
         send(2, c)
+    loads[-1].wait()
+    g_rest, m_rest, v_rest = (
+        [x[top + r : top + r + 1, :] for r in range(rest)] for x in (g_buf, m_buf, v_buf)
+    )
+
+    def packed(row):
+        return jnp.concatenate(
+            [row[:, b * BLOCK : (b + 1) * BLOCK] for b in range(blocks_dev)], axis=0
+        )
+
+    for r in range(rest):
+        kept = keep[0] > 0
+        tails[0][r, 0:blocks_dev, :] = packed(p_rest[r : r + 1, :])
+        clipped = clip_factor * packed(g_rest[r])
+        first = beta_one * packed(m_rest[r]) + (1.0 - beta_one) * clipped
+        tails[1][r, 0:blocks_dev, :] = jnp.where(kept, first, 0.0)
+        second = beta_two * packed(v_rest[r]) + (1.0 - beta_two) * clipped * clipped
+        tails[2][r, 0:blocks_dev, :] = jnp.where(kept, second, 0.0)
+    for a in range(3):
+        send(a, n_piece)
 
     @pl.when(has_up)
     def _():
@@ -213,7 +242,7 @@
     to_scalar = pltpu.make_async_copy(where_v, where_s, where_sem)
     to_scalar.start()
     to_scalar.wait()
-    for c in loads[4:]:
+    for c in loads[4:-1]:
         c.wait()
 
     def relay(a, c):
@@ -230,48 +259,61 @@
 
     correct_one = 1.0 - beta_one**STEP
     correct_two = 1.0 - beta_two**STEP
-    outs = []
-    for c in range(n_piece):
-        relay(1, c)
-        relay(2, c)
+    def finish(j, valid, rows, old, first, second):
+        dst = (rows, pl.ds(j * BLOCK, BLOCK))
+        updated = old - learn_rate * (first / correct_one) / (
+            jnp.sqrt(second / correct_two) + adam_eps
+        )
+        o_p[dst] = jnp.where(valid & (second > 0.0), updated, 0.0)
+        o_m[dst] = jnp.where(valid, first, 0.0)
+        o_v[dst] = jnp.where(valid, second, 0.0)
+
+    for c in range(n_piece + 1):
+        for a in range(3):
+            if a > 0 or c == n_piece:
+                relay(a, c)
         for a in range(3):
             pl.when(is_even | has_up)(near_own(a, c).wait_recv)
-        rows = span(c)
         for j in range(blocks_dev):
             block = where_s[j, 0]
             valid = block < total_blocks
-            start = jnp.where(valid, block, 0) * BLOCK
-            dst = (rows, pl.ds(j * BLOCK, BLOCK))
-            old, first, second = (windows[a][c][:, pl.ds(start, BLOCK)] for a in range(3))
-            updated = old - learn_rate * (first / correct_one) / (
-                jnp.sqrt(second / correct_two) + adam_eps
-            )
-            o_p[dst] = jnp.where(valid & (second > 0.0), updated, 0.0)
-            o_m[dst] = jnp.where(valid, first, 0.0)
-            o_v[dst] = jnp.where(valid, second, 0.0)
-        for a, (buf, hbm) in enumerate(((o_p, op_hbm), (o_m, om_hbm), (o_v, ov_hbm))):
-            outs.append(
-                pltpu.make_async_copy(buf.at[rows], hbm.at[rows], out_sem.at[a * n_piece + c])
-            )
-            outs[-1].start()
+            block = jnp.where(valid, block, 0)
+            if c < n_piece:
+                took = [windows[a][c][:, pl.ds(block * BLOCK, BLOCK)] for a in range(3)]
+                finish(j, valid, span(c), *took)
+            else:
+                took = [
+                    jnp.concatenate([tails[a][r, pl.ds(block, 1), :] for r in range(rest)], axis=0)
+                    for a in range(3)
+                ]
+                finish(j, valid, pl.ds(top, rest), *took)
 
     @pl.when(has_down)
     def _():
         far_keep.wait_send()
         for a in range(3):
-            for c in range(n_piece):
+            for c in range(n_piece + 1):
                 far_copy(a, c).wait_send()
 
     @pl.when(is_odd | has_up)
     def _():
         near_keep.wait_send()
         for a in range(3):
-            for c in range(n_piece):
+            for c in range(n_piece + 1):
                 near_own(a, c).wait_send()
 
     for c in ag_copies:
         c.wait_send()
-    for c in outs:
+
+
+def put_kernel(a_in, b_in, c_in, a_out, b_out, c_out, sem):
+    copies = [
+        pltpu.make_async_copy(src, dst, sem.at[i])
+        for i, (src, dst) in enumerate(((a_in, a_out), (b_in, b_out), (c_in, c_out)))
+    ]
+    for c in copies:
+        c.start()
+    for c in copies:
         c.wait()
 
 
@@ -280,21 +322,23 @@
     blocks_dev = rows_dev // BLOCK
     sizes = tuple(lax.axis_size(a) for a in AXES)
     assert DROPS <= 2 * blocks_dev and sizes[2] % 2 == 0
-    step = 16
-    pieces = [(r, min(step, features - r)) for r in range(0, features, step)]
+    pieces = [(r, ROWS) for r in range(0, features - ROWS + 1, ROWS)]
+    rest = features % ROWS
+    assert rest and (rest * blocks_dev) % ROWS == 0
     full = jax.ShapeDtypeStruct((features, rows_dev), jnp.float32)
     plain = pltpu.VMEM((features, rows_dev), jnp.float32)
     window = [pltpu.VMEM((rows, 3 * rows_dev), jnp.float32) for _, rows in pieces]
+    tail = pltpu.VMEM((rest, 3 * blocks_dev, BLOCK), jnp.float32)
     n_piece = len(pieces)
     n_ag = 2 * (sum(sizes) - 3)
     any_spec = pl.BlockSpec(memory_space=pl.ANY)
     p1, m1, v1, rms = pl.pallas_call(
         functools.partial(kernel, sizes, pieces),
         out_shape=(full, full, full, jax.ShapeDtypeStruct((1, 1), jnp.float32)),
-        in_specs=[any_spec] * 5,
-        out_specs=(any_spec, any_spec, any_spec, pl.BlockSpec(memory_space=pltpu.VMEM)),
+        in_specs=[pl.BlockSpec(memory_space=pltpu.HBM)] * 5,
+        out_specs=(pl.BlockSpec(memory_space=pltpu.VMEM),) * 4,
         scratch_shapes=[
-            [window, window, window], plain, plain, plain, plain, plain, plain,
+            [window, window, window], [tail, tail, tail], plain, plain, plain, pltpu.VMEM((rest, rows_dev), jnp.float32),
             pltpu.VMEM((3, blocks_dev, BLOCK), jnp.int32),
             pltpu.VMEM((sizes[0], 8, BLOCK), jnp.float32),
             pltpu.VMEM((sizes[1], 8, BLOCK), jnp.float32),
@@ -304,12 +348,11 @@
             pltpu.VMEM((sizes[2], 8, BLOCK), jnp.int32),
             pltpu.VMEM((blocks_dev, BLOCK), jnp.int32),
             pltpu.SMEM((blocks_dev, BLOCK), jnp.int32),
-            pltpu.SemaphoreType.DMA((4 + n_piece,)),
-            pltpu.SemaphoreType.DMA((3 * n_piece,)),
-            pltpu.SemaphoreType.DMA((3 * n_piece + 1,)),
-            pltpu.SemaphoreType.DMA((3 * n_piece + 1,)),
-            pltpu.SemaphoreType.DMA((3 * n_piece + 1,)),
-            pltpu.SemaphoreType.DMA((3 * n_piece + 1,)),
+            pltpu.SemaphoreType.DMA((5 + n_piece,)),
+            pltpu.SemaphoreType.DMA((3 * n_piece + 4,)),
+            pltpu.SemaphoreType.DMA((3 * n_piece + 4,)),
+            pltpu.SemaphoreType.DMA((3 * n_piece + 4,)),
+            pltpu.SemaphoreType.DMA((3 * n_piece + 4,)),
             pltpu.SemaphoreType.DMA((n_ag,)),
             pltpu.SemaphoreType.DMA((n_ag,)),
             pltpu.SemaphoreType.DMA,
@@ -317,7 +360,14 @@
         compiler_params=pltpu.CompilerParams(
             collective_id=0, has_side_effects=True, vmem_limit_bytes=40 * 1024 * 1024
         ),
-    )(params, gradients, moment_one, moment_two, keep_mask.reshape(blocks_dev, BLOCK))
+    )(*(pltpu.with_memory_space_constraint(x, pltpu.HBM) for x in (params, gradients, moment_one, moment_two, keep_mask.reshape(blocks_dev, BLOCK))))
+    p1, m1, v1 = pl.pallas_call(
+        put_kernel,
+        out_shape=(full, full, full),
+        in_specs=[pl.BlockSpec(memory_space=pltpu.VMEM)] * 3,
+        out_specs=(pl.BlockSpec(memory_space=pltpu.HBM),) * 3,
+        scratch_shapes=[pltpu.SemaphoreType.DMA((3,))],
+    )(*(pltpu.with_memory_space_constraint(x, pltpu.VMEM) for x in (p1, m1, v1)))
     return p1, m1, v1, rms.reshape(())
 
 

time: 57.5 us -> 47.2 us (0.82)
  local copies, waits for them, and re-layouts: 7.24 us -> 0 us
  Pallas kernels: 47.6 us -> 43.9 us
    unnamed x13 -> x0, local copies, waits for them, and re-layouts: 7.24 us -> none
    pallas_call x1, Pallas kernels: 47.6 us -> 42.8 us  [shards(): pl.pallas_call(functools.partial(kernel, sizes, pieces), out_shape=(full,...]
    pallas_call x0 -> x1, Pallas kernels: none -> 1.17 us  [shards(): pl.pallas_call(put_kernel, out_shape=(full, full, full), in_specs=[pl.Blo...]
where the time goes in v2:
time: 47.2 us; the launch traced here: 46.3 us
  Pallas kernels  43.9 us (93%)
  between operations  2.41 us (5%)
    pallas_call x1, Pallas kernels, shards(): pl.pallas_call(functools.partial(kernel, sizes, pieces), out_shape=(full,...  42.8 us
    pallas_call x1, Pallas kernels, shards(): pl.pallas_call(put_kernel, out_shape=(full, full, full), in_specs=[pl.Blo...  1.17 us

profile of v2, /device:TPU:5, one launch (start us, length us, event | category | flops | bytes accessed | tf_op | source)
XLA Modules:
  0.0 46.3 jit_solution(2480721794928530036)
XLA Ops:
  0.6 42.8 %shard_map.84 = (f32[59,2048]{1,0:T(8,128)S(1)}, f32[59,2048]{1,0:T(8,128)S(1)}, f32[59,2048]{1,0:T(8,128)S(1)}, f32[1,1]{1,0:T(1,128)}) custom-call(f32[59,2048]{1,0:T(8,128)} %p_hbm.1, f32[59,2048]{1,0:T(8,128)} %g_hbm.1, f32[59,2048]{1,0:T(8,128)} %m_hbm.1, f32[59,2048]{1,0:T(8,128)} %v_hbm.1, s32[16,128]{1,0:T(8,128)} %bitcast.2), custom_call_target="tpu_custom_call" | custom-call | tf_op jit(solution)/shard_map/pallas_call | solution.py:335
  43.4 1.2 %shard_map.85 = (f32[59,2048]{1,0:T(8,128)}, f32[59,2048]{1,0:T(8,128)}, f32[59,2048]{1,0:T(8,128)}) custom-call(f32[59,2048]{1,0:T(8,128)S(1)} %get-tuple-element.11.a_in, f32[59,2048]{1,0:T(8,128)S(1)} %get-tuple-element.12.b_in, f32[59,2048]{1,0:T(8,128)S(1)} %get-tuple-element.13.c_in), custom_call_target="tpu_custom_call" | custom-call | tf_op jit(solution)/shard_map/pallas_call | solution.py:364

commit v3 on v2

--- a/solution.py
+++ b/solution.py
@@ -23,7 +23,7 @@
 
 def kernel(
     sizes, pieces, p_hbm, g_hbm, m_hbm, v_hbm, k_hbm, o_p, o_m, o_v, rms_ref,
-    windows, tails, g_buf, m_buf, v_buf, p_rest, keep, ag_x, ag_y, ag_z, ct_x, ct_y, ct_z,
+    windows, tails, g_buf, m_buf, v_buf, p_rest, keep, ag_x, ag_y, ct_x, ct_y,
     where_v, where_s, load_sem, far_send, far_recv, near_send, near_recv,
     ag_send, ag_recv, where_sem,
 ):
@@ -73,8 +73,7 @@
         pl.semaphore_signal(barrier, inc=1, device_id=device, device_id_type=MESH)
 
     groups = (
-        (iz, nz, ag_z, ct_z, lambda i: (ix, iy, i)),
-        (iy, ny, ag_y, ct_y, lambda i: (ix, i, iz)),
+        (iy * nz + iz, ny * nz, ag_y, ct_y, lambda i: (ix, lax.div(i, nz), lax.rem(i, nz))),
         (ix, nx, ag_x, ct_x, lambda i: (i, iy, iz)),
     )
     greet(partner)
@@ -95,7 +94,7 @@
 
     pl.semaphore_wait(
         barrier,
-        1 + (nx - 1) + (ny - 1) + (nz - 1) + has_up.astype(jnp.int32) + has_down.astype(jnp.int32),
+        1 + (nx - 1) + (ny * nz - 1) + has_up.astype(jnp.int32) + has_down.astype(jnp.int32),
     )
 
     def far(i, src, dst):
@@ -165,7 +164,7 @@
                 )
                 copies[-1].start()
                 sem_at += 1
-        for _ in range(1 if phase < 2 else n_piece):
+        for _ in range((2, n_piece)[phase]):
             if flow:
                 send(0, flow.pop(0))
         for c in copies:
@@ -322,7 +321,9 @@
     blocks_dev = rows_dev // BLOCK
     sizes = tuple(lax.axis_size(a) for a in AXES)
     assert DROPS <= 2 * blocks_dev and sizes[2] % 2 == 0
-    pieces = [(r, ROWS) for r in range(0, features - ROWS + 1, ROWS)]
+    whole = features // ROWS
+    widths = [1] * whole if whole < 4 else [2] + [1] * (whole - 4) + [2]
+    pieces = [(sum(widths[:i]) * ROWS, w * ROWS) for i, w in enumerate(widths)]
     rest = features % ROWS
     assert rest and (rest * blocks_dev) % ROWS == 0
     full = jax.ShapeDtypeStruct((features, rows_dev), jnp.float32)
@@ -330,7 +331,7 @@
     window = [pltpu.VMEM((rows, 3 * rows_dev), jnp.float32) for _, rows in pieces]
     tail = pltpu.VMEM((rest, 3 * blocks_dev, BLOCK), jnp.float32)
     n_piece = len(pieces)
-    n_ag = 2 * (sum(sizes) - 3)
+    n_ag = 2 * (sizes[0] - 1 + sizes[1] * sizes[2] - 1)
     any_spec = pl.BlockSpec(memory_space=pl.ANY)
     p1, m1, v1, rms = pl.pallas_call(
         functools.partial(kernel, sizes, pieces),
@@ -341,11 +342,9 @@
             [window, window, window], [tail, tail, tail], plain, plain, plain, pltpu.VMEM((rest, rows_dev), jnp.float32),
             pltpu.VMEM((3, blocks_dev, BLOCK), jnp.int32),
             pltpu.VMEM((sizes[0], 8, BLOCK), jnp.float32),
-            pltpu.VMEM((sizes[1], 8, BLOCK), jnp.float32),
-            pltpu.VMEM((sizes[2], 8, BLOCK), jnp.float32),
+            pltpu.VMEM((sizes[1] * sizes[2], 8, BLOCK), jnp.float32),
             pltpu.VMEM((sizes[0], 8, BLOCK), jnp.int32),
-            pltpu.VMEM((sizes[1], 8, BLOCK), jnp.int32),
-            pltpu.VMEM((sizes[2], 8, BLOCK), jnp.int32),
+            pltpu.VMEM((sizes[1] * sizes[2], 8, BLOCK), jnp.int32),
             pltpu.VMEM((blocks_dev, BLOCK), jnp.int32),
             pltpu.SMEM((blocks_dev, BLOCK), jnp.int32),
             pltpu.SemaphoreType.DMA((5 + n_piece,)),

time: 47.2 us -> 46.4 us (0.983); the launches traced: 46.3 us -> 46.3 us
  no operation moved by 1% of the time
where the time goes in v3:
time: 46.4 us; the launch traced here: 46.3 us
  Pallas kernels  43.9 us (95%)
  between operations  2.41 us (5%)
    pallas_call x1, Pallas kernels, shards(): pl.pallas_call(functools.partial(kernel, sizes, pieces), out_shape=(full,...  42.7 us
    pallas_call x1, Pallas kernels, shards(): pl.pallas_call(put_kernel, out_shape=(full, full, full), in_specs=[pl.Blo...  1.17 us

profile of v3, /device:TPU:5, one launch (start us, length us, event | category | flops | bytes accessed | tf_op | source)
XLA Modules:
  0.0 46.3 jit_solution(13553143432672228768)
XLA Ops:
  0.6 42.7 %shard_map.84 = (f32[59,2048]{1,0:T(8,128)S(1)}, f32[59,2048]{1,0:T(8,128)S(1)}, f32[59,2048]{1,0:T(8,128)S(1)}, f32[1,1]{1,0:T(1,128)}) custom-call(f32[59,2048]{1,0:T(8,128)} %p_hbm.1, f32[59,2048]{1,0:T(8,128)} %g_hbm.1, f32[59,2048]{1,0:T(8,128)} %m_hbm.1, f32[59,2048]{1,0:T(8,128)} %v_hbm.1, s32[16,128]{1,0:T(8,128)} %bitcast.2), custom_call_target="tpu_custom_call" | custom-call | tf_op jit(solution)/shard_map/pallas_call | solution.py:336
  43.3 1.2 %shard_map.85 = (f32[59,2048]{1,0:T(8,128)}, f32[59,2048]{1,0:T(8,128)}, f32[59,2048]{1,0:T(8,128)}) custom-call(f32[59,2048]{1,0:T(8,128)S(1)} %get-tuple-element.11.a_in, f32[59,2048]{1,0:T(8,128)S(1)} %get-tuple-element.12.b_in, f32[59,2048]{1,0:T(8,128)S(1)} %get-tuple-element.13.c_in), custom_call_target="tpu_custom_call" | custom-call | tf_op jit(solution)/shard_map/pallas_call | solution.py:363
